TPU v7x, 256 devices: a whole 4x4x8 slice. The times are simulated.
256 devices in a mesh: space: 32 (over x_lo, z, core), src: 8 (over y, x_hi).
Axes of the slice: x: 4 (x_hi: 2, x_lo: 2; x = x_hi * 2 + x_lo), y: 4, z: 8, core: 2. Of those that a mesh axis runs over, the one named last changes fastest.
Arguments:
- medium: float32 [32, 64, 64, 64], P('space'), may hold values from 0.8 to 1.2
- source_cells: int32 [8, 4096], P('src'), may hold values from 0 to 8388607, as said below
- source_weights: float32 [2, 8, 4096], P(None, 'src'), may hold values from -48 to 48
- adjoint: bfloat16 [2, 8, 32, 64, 64, 64], P(None, 'src', 'space'), may hold values from -6 to 6
Outputs:
- field: float32 [2, 8, 32, 64, 64, 64], P(None, 'src', 'space')
- gradient: float32 [32, 64, 64, 64], P('space', 'src')
Inputs may be any that keep to these rules, and one draw needn't show every extreme that they name: source_cells[s, p] is the cell b * 64**3 + (x * 64 + y) * 64 + z of the point p of source s; points may repeat and fall in any box.
All inputs are finite; a program needn't handle non-finite values.
Results may differ from a plain program's by a relative error of at most 0.0003.
Values sent between devices are 32-bit elements; how exact they have to be, the bound alone decides.
A program may use at most 128 MiB of HBM per device.

v0:
```python
import jax
import jax.numpy as jnp
from jax import lax
from jax.sharding import PartitionSpec as P

TERMS = 2
BGX = 2
BGZ = 4


wave_sq = 1.0
damping = 0.25
highest = lax.Precision.HIGHEST


def shifted_2(block, axis, distance):
    devices = range(lax.axis_size(axis))
    route = [(i - distance, i) for i in devices if i - distance in devices]
    return lax.ppermute(block, axis, route)


def dft_tables(length):
    positions = jnp.arange(length, dtype=jnp.int32)
    product = positions[:, None] * positions[None, :] % length
    phases = 2.0 * jnp.pi / length * product.astype(jnp.float32)
    return (jnp.cos(phases), jnp.sin(phases))


def complex_matrix(tables, orientation):
    cosines, sines = tables
    upper = jnp.stack([cosines, orientation * sines])
    lower = jnp.stack([-orientation * sines, cosines])
    return jnp.stack([upper, lower])


def spectral_kernel(length):
    frequency = jnp.arange(length, dtype=jnp.float32)
    eigenvalue = 2.0 - 2.0 * jnp.cos(2.0 * jnp.pi / length * frequency)
    summed = eigenvalue[:, None, None] + eigenvalue[None, :, None] + eigenvalue[None, None, :]
    shifted = summed - wave_sq
    scaling = 1.0 / ((shifted * shifted + damping * damping) * float(length) ** 3)
    return (shifted * scaling, damping * scaling)


def transform(values, matrix):
    for dimension in range(3):
        values = jnp.einsum(
            "pqkn,qsnbc->psbck",
            matrix,
            values,
            precision=highest,
            preferred_element_type=jnp.float32,
        )
    return values


def times_gamma(values, ratio):
    return jnp.stack([values[0] - ratio * values[1], values[1] + ratio * values[0]])


def finish_green(spectrum, inverse_matrix, kernel):
    kernel_real, kernel_imag = kernel
    product = jnp.stack(
        [
            spectrum[0] * kernel_real - spectrum[1] * kernel_imag,
            spectrum[0] * kernel_imag + spectrum[1] * kernel_real,
        ]
    )
    return transform(product, inverse_matrix)


def exchange_faces(packed, strides, box_coords, extents):
    last_cell = packed.shape[2] - 1
    corrections = []
    for dimension in range(3):
        lower_plane = lax.index_in_dim(packed, 0, dimension + 2, keepdims=False)
        upper_plane = lax.index_in_dim(packed, last_cell, dimension + 2, keepdims=False)
        face_pair = []
        for offset, face_plane, edge_coord in (
            (strides[dimension], upper_plane, 0),
            (-strides[dimension], lower_plane, extents[dimension] - 1),
        ):
            arrived = shifted_2(face_plane, "space", offset)
            keep_mask = (box_coords[dimension] != edge_coord).astype(jnp.float32)
            face_pair.append(keep_mask * arrived - face_plane)
        corrections.append(face_pair)
    return corrections


def face_field(corrections, length):
    filled = 0.0
    last_cell = length - 1
    for dimension in range(3):
        dims_shape = [1, 1, 1, 1, 1]
        dims_shape[dimension + 2] = length
        positions = jnp.arange(length, dtype=jnp.int32).reshape(dims_shape)
        lower_mask = (positions == 0).astype(jnp.float32)
        upper_mask = (positions == last_cell).astype(jnp.float32)
        lower_face = jnp.expand_dims(corrections[dimension][0], dimension + 2)
        upper_face = jnp.expand_dims(corrections[dimension][1], dimension + 2)
        filled = filled + lower_mask * lower_face + upper_mask * upper_face
    return filled


def local(medium, source_cells, source_weights, adjoint):
    edge_cells = medium.shape[1]
    sources = source_cells.shape[0]
    across = lax.axis_size("space") // 8
    box_index = lax.axis_index("space")
    box_coords = (box_index // (BGZ * across), box_index // BGZ % across, box_index % BGZ)
    strides = (across * BGZ, BGZ, 1)
    extents = (BGX, across, BGZ)
    tables = dft_tables(edge_cells)
    forward_matrix = complex_matrix(tables, 1.0)
    inverse_matrix = complex_matrix(tables, -1.0)
    kernel = spectral_kernel(edge_cells)
    cube = edge_cells**3
    local_cell = source_cells - box_index * cube
    inside = (local_cell >= 0) & (local_cell < cube)
    segment_ids = (
        jnp.where(inside, local_cell, cube)
        + (cube + 1) * jnp.arange(sources, dtype=jnp.int32)[:, None]
    )

    def place(weights):
        summed = jax.ops.segment_sum(
            weights.reshape(-1), segment_ids.reshape(-1), num_segments=sources * (cube + 1)
        )
        return summed.reshape(sources, cube + 1)[:, :cube].reshape(
            sources, edge_cells, edge_cells, edge_cells
        )

    source = jnp.stack([place(source_weights[0]), place(source_weights[1])])
    potential = medium[0] - wave_sq
    ratio = potential / damping
    field = times_gamma(
        finish_green(transform(source, forward_matrix), inverse_matrix, kernel), ratio
    )
    for term_index in range(TERMS):
        corrections = exchange_faces(field, strides, box_coords, extents)
        drive = potential * field + damping * jnp.stack([field[1], -field[0]]) + source
        spectrum = transform(drive + face_field(corrections, edge_cells), forward_matrix)
        update = field - finish_green(spectrum, inverse_matrix, kernel)
        field = field - times_gamma(update, ratio)
    adjoint_full = adjoint[:, :, 0].astype(jnp.float32)
    partial_sum = jnp.sum(adjoint_full[0] * field[0] - adjoint_full[1] * field[1], axis=0)
    owned = lax.psum_scatter(partial_sum, "src", scatter_dimension=0, tiled=True)
    return (field[:, :, None], owned[None])


def solution(mesh):
    placed = (
        P("space", None, None, None),
        P("src", None),
        P(None, "src", None),
        P(None, "src", "space", None, None, None),
    )
    return jax.shard_map(
        local,
        mesh=mesh,
        in_specs=placed,
        out_specs=(P(None, "src", "space", None, None, None), P("space", "src", None, None)),
        check_vma=False,
    )
```

profile of v0, /device:TPU:1, one launch (start us, length us, event | category | flops | bytes accessed | tf_op | source)
XLA Modules:
  0.0 465.8 jit_solution(11203267550183170410)
XLA Ops:
  9.0 28.1 %scatter_custom_fusion = f32[262145]{0:T(1024)S(1)} fusion(s32[4096]{0:T(1024)S(1)} %bitcast.403, f32[4096]{0:T(1024)S(1)} %bitcast.406, f32[]{:T(128)} %constant.75.clone.1), kind=kCustom, calls=%fused_computation.131 | custom fusion | flops 4096 | bytes 1048584 | tf_op jit(solution)/shard_map/scatter-add | solution.py:126
  37.1 5.6 %reshape.768 = f32[1,262145]{1,0:T(1,128)} reshape(f32[262145]{0:T(1024)S(1)} %scatter_custom_fusion) | data formatting | bytes 2097160 | tf_op jit(solution)/shard_map/reshape | solution.py:129
  42.8 28.3 %scatter_custom_fusion.1 = f32[262145]{0:T(1024)S(1)} fusion(s32[4096]{0:T(1024)S(1)} %bitcast.404, f32[4096]{0:T(1024)S(1)} %bitcast.405, f32[]{:T(128)} %constant.75.clone.1), kind=kCustom, calls=%fused_computation.129 | custom fusion | flops 4096 | bytes 1048584 | tf_op jit(solution)/shard_map/scatter-add | solution.py:126
  71.1 4.9 %reshape.769 = f32[1,262145]{1,0:T(1,128)S(1)} reshape(f32[262145]{0:T(1024)S(1)} %scatter_custom_fusion.1) | data formatting | bytes 2097160 | tf_op jit(solution)/shard_map/reshape | solution.py:129
  76.0 16.3 %fusion.143 = (f32[1,262144]{1,0:T(1,128)S(1)}, f32[262144]{0:T(1024)}, f32[262144]{0:T(1024)}, f32[1,262144]{1,0:T(1,128)}) fusion(f32[1,262145]{1,0:T(1,128)S(1)} %reshape.769, f32[1,262145]{1,0:T(1,128)} %reshape.768), kind=kLoop, calls=%fused_computation.200 | loop fusion | bytes 6291456 | tf_op jit(solution)/shard_map/slice | solution.py:129
  93.9 2.2 copy.58
  97.7 2.2 copy.59
  100.0 6.2 %fusion.96 = f32[2,64,64,64,1]{3,2,0,1,4:T(8,128)S(1)} fusion(f32[1,1,64,64,64]{2,4,0,3,1:T(8,128)} %copy.59, f32[1,1,64,64,64]{2,4,0,3,1:T(8,128)} %copy.58, f32[1,2,64,64]{3,2,1,0:T(8,128)S(1)} %get-tuple-element.39, f32[1,2,64,64]{3,2,1,0:T(8,128)S(1)} %get-tuple-element.42), kind=kOutput, calls=%fused_computation.96 | convolution fusion | flops 805847040 | bytes 4259840 | tf_op jit(solution)/shard_map/pqkn,qsnbc->psbck/dot_general | solution.py:47
  106.2 8.7 %fusion.51 = f32[2,64,64,64,1]{3,2,0,1,4:T(8,128)S(1)} fusion(f32[2,64,64,64,1]{3,2,0,1,4:T(8,128)S(1)} %fusion.96, f32[1,2,64,64]{3,2,1,0:T(8,128)S(1)} %get-tuple-element.39, f32[1,2,64,64]{3,2,1,0:T(8,128)S(1)} %get-tuple-element.42), kind=kOutput, calls=%fused_computation.81 | convolution fusion | flops 805322752 | bytes 4259840 | tf_op jit(solution)/shard_map/pqkn,qsnbc->psbck/dot_general | solution.py:47
  114.9 9.2 %fusion.54 = f32[2,1,64,64,64]{4,3,0,2,1:T(8,128)S(1)} fusion(f32[2,64,64,64,1]{3,2,0,1,4:T(8,128)S(1)} %fusion.51, f32[1,2,64,64]{3,2,1,0:T(8,128)S(1)} %get-tuple-element.39, f32[1,2,64,64]{3,2,1,0:T(8,128)S(1)} %get-tuple-element.42), kind=kOutput, calls=%fused_computation.82 | convolution fusion | flops 805322752 | bytes 4259840 | tf_op jit(solution)/shard_map/pqkn,qsnbc->psbck/dot_general | solution.py:47
  126.0 8.6 %fusion.57 = f32[2,64,64,64,1]{3,2,0,1,4:T(8,128)S(1)} fusion(f32[2,64,64,64,1]{3,2,0,1,4:T(8,128)S(1)} %maximum_bitcast_fusion.2, f32[1,2,64,64]{3,2,1,0:T(8,128)S(1)} %get-tuple-element.43, f32[1,2,64,64]{3,2,1,0:T(8,128)S(1)} %get-tuple-element.38), kind=kOutput, calls=%fused_computation.83 | convolution fusion | flops 805322752 | bytes 4259840 | tf_op jit(solution)/shard_map/pqkn,qsnbc->psbck/dot_general | solution.py:47
  134.7 9.1 %fusion.60 = f32[2,64,64,64,1]{3,2,0,1,4:T(8,128)S(1)} fusion(f32[2,64,64,64,1]{3,2,0,1,4:T(8,128)S(1)} %fusion.57, f32[1,2,64,64]{3,2,1,0:T(8,128)S(1)} %get-tuple-element.43, f32[1,2,64,64]{3,2,1,0:T(8,128)S(1)} %get-tuple-element.38), kind=kOutput, calls=%fused_computation.84 | convolution fusion | flops 805322752 | bytes 4259840 | tf_op jit(solution)/shard_map/pqkn,qsnbc->psbck/dot_general | solution.py:47
  143.8 8.6 %fusion.63 = f32[2,1,64,64,64]{4,3,0,2,1:T(8,128)S(1)} fusion(f32[2,64,64,64,1]{3,2,0,1,4:T(8,128)S(1)} %fusion.60, f32[1,2,64,64]{3,2,1,0:T(8,128)S(1)} %get-tuple-element.43, f32[1,2,64,64]{3,2,1,0:T(8,128)S(1)} %get-tuple-element.38), kind=kOutput, calls=%fused_computation.85 | convolution fusion | flops 805322752 | bytes 4259840 | tf_op jit(solution)/shard_map/pqkn,qsnbc->psbck/dot_general | solution.py:47
  152.3 3.7 fusion.141
  156.7 4.6 collective-permute-start
  163.4 5.7 %collective-permute-start.2 = (f32[2,1,64,64]{3,2,0,1:T(8,128)}, f32[2,1,64,64]{3,2,0,1:T(8,128)}, u32[]{:S(2)}, u32[]{:S(2)}) collective-permute-start(f32[2,1,64,64]{3,2,0,1:T(8,128)} %bitcast.59), channel_id=1, source_target_pairs={{0,32},{8,40},{16,48},{24,56},{32,64},{40,72},{48,80},{56,88},{64,... | collective-permute-start | bytes 98312 | tf_op jit(solution)/shard_map/ppermute | solution.py:19
  170.4 4.4 fusion.1
  174.7 4.6 collective-permute-start.4
  179.3 2.7 stack.143
  182.0 3.2 constant_dynamic-update-slice_fusion.1
  186.9 3.2 constant_dynamic-update-slice_fusion
  190.0 4.2 convert_element_type.143
  200.6 5.5 %fusion.11 = f32[2,64,64,64,1]{3,2,1,0,4:T(8,128)S(1)} fusion(f32[2,64,64,64]{3,2,1,0:T(8,128)S(1)} %copy-done.9, f32[1,64,64,64]{3,2,1,0:T(8,128)} %get-tuple-element.6, f32[1,64,64,64]{3,2,1,0:T(8,128)S(1)} %copy-done.1, f32[1,64,64,64]{3,2,1,0:T(8,128)S(1)} %get-tuple-element.7, f32[2,64,64]{2,1,0:T(8,128)S(1)} %subtract_bitcast_fusion.6, ...), kind=kLoop, calls=%fused_computation.33 | loop fusion | flops 9437184 | bytes 8585728 | tf_op jit(solution)/shard_map/add | solution.py:142
  206.1 8.7 %fusion.66 = f32[2,64,64,64,1]{3,2,0,1,4:T(8,128)S(1)} fusion(f32[2,64,64,64,1]{3,2,1,0,4:T(8,128)S(1)} %fusion.11, f32[1,2,64,64]{3,2,1,0:T(8,128)S(1)} %get-tuple-element.39, f32[1,2,64,64]{3,2,1,0:T(8,128)S(1)} %get-tuple-element.42), kind=kOutput, calls=%fused_computation.86 | convolution fusion | flops 805322752 | bytes 4259840 | tf_op jit(solution)/shard_map/pqkn,qsnbc->psbck/dot_general | solution.py:47
  214.8 9.1 %fusion.69 = f32[2,64,64,64,1]{3,2,0,1,4:T(8,128)S(1)} fusion(f32[2,64,64,64,1]{3,2,0,1,4:T(8,128)S(1)} %fusion.66, f32[1,2,64,64]{3,2,1,0:T(8,128)S(1)} %get-tuple-element.39, f32[1,2,64,64]{3,2,1,0:T(8,128)S(1)} %get-tuple-element.42), kind=kOutput, calls=%fused_computation.87 | convolution fusion | flops 805322752 | bytes 4259840 | tf_op jit(solution)/shard_map/pqkn,qsnbc->psbck/dot_general | solution.py:47
  223.9 8.9 %fusion.72 = f32[2,1,64,64,64]{4,3,0,2,1:T(8,128)S(1)} fusion(f32[2,64,64,64,1]{3,2,0,1,4:T(8,128)S(1)} %fusion.69, f32[1,2,64,64]{3,2,1,0:T(8,128)S(1)} %get-tuple-element.39, f32[1,2,64,64]{3,2,1,0:T(8,128)S(1)} %get-tuple-element.42), kind=kOutput, calls=%fused_computation.88 | convolution fusion | flops 805322752 | bytes 4259840 | tf_op jit(solution)/shard_map/pqkn,qsnbc->psbck/dot_general | solution.py:47
  234.8 8.7 %fusion.75 = f32[2,64,64,64,1]{3,2,0,1,4:T(8,128)S(1)} fusion(f32[2,64,64,64,1]{3,2,0,1,4:T(8,128)S(1)} %maximum_bitcast_fusion.3, f32[1,2,64,64]{3,2,1,0:T(8,128)S(1)} %get-tuple-element.43, f32[1,2,64,64]{3,2,1,0:T(8,128)S(1)} %get-tuple-element.38), kind=kOutput, calls=%fused_computation.89 | convolution fusion | flops 805322752 | bytes 4259840 | tf_op jit(solution)/shard_map/pqkn,qsnbc->psbck/dot_general | solution.py:47
  243.5 12.0 %fusion.78 = f32[2,64,64,64]{3,2,0,1:T(8,128)} fusion(f32[2,64,64,64,1]{3,2,0,1,4:T(8,128)S(1)} %fusion.75, f32[1,2,64,64]{3,2,1,0:T(8,128)S(1)} %get-tuple-element.43, f32[1,2,64,64]{3,2,1,0:T(8,128)S(1)} %get-tuple-element.38), kind=kOutput, calls=%fused_computation.90 | convolution fusion | flops 805322752 | bytes 4259840 | tf_op jit(solution)/shard_map/pqkn,qsnbc->psbck/dot_general | solution.py:47
  255.5 5.6 %copy.71 = f32[2,64,64,64]{1,3,0,2:T(8,128)} copy(f32[2,64,64,64]{3,2,0,1:T(8,128)} %fusion.78) | data formatting | bytes 4194304 | tf_op jit(solution)/shard_map/reshape.47
  261.1 7.1 %bitcast_subtract_fusion.1 = f32[2,1,64,64,64]{4,3,2,1,0:T(8,128)S(1)} fusion(f32[1,1,64,64,64]{4,3,2,1,0:T(8,128)} %bitcast.384, f32[1,1,64,64,64]{4,3,2,1,0:T(8,128)S(1)} %bitcast.377, f32[2,64,64,64]{1,3,0,2:T(8,128)} %copy.71, f32[1,2,64,64]{3,2,1,0:T(8,128)S(1)} %get-tuple-element.43, f32[1,2,64,64]{3,2,1,0:T(8,128)S(1)} %get-tuple-element.38), kind=kOutput, calls=%fused_computation.46 | convolution fusion | flops 806371328 | bytes 6356992 | tf_op jit(solution)/shard_map/pqkn,qsnbc->psbck/dot_general | solution.py:47
  271.3 3.3 slice_reduce_fusion.1
  275.1 5.8 %collective-permute-start.8 = (f32[2,1,64,64]{3,2,0,1:T(8,128)S(1)}, f32[2,1,64,64]{3,2,0,1:T(8,128)S(1)}, u32[]{:S(2)}, u32[]{:S(2)}) collective-permute-start(f32[2,1,64,64]{3,2,0,1:T(8,128)S(1)} %bitcast.401), channel_id=1, source_target_pairs={{0,32},{8,40},{16,48},{24,56},{32,64},{40,72},{48,80},{56,88},{64,... | collective-permute-start | bytes 98312 | tf_op jit(solution)/shard_map/ppermute | solution.py:19
  280.9 4.9 %collective-permute-start.6 = (f32[2,1,64,64]{3,2,0,1:T(8,128)S(1)}, f32[2,1,64,64]{3,2,0,1:T(8,128)S(1)}, u32[]{:S(2)}, u32[]{:S(2)}) collective-permute-start(f32[2,1,64,64]{3,2,0,1:T(8,128)S(1)} %get-tuple-element.23), channel_id=1, source_target_pairs={{0,128},{8,136},{16,144},{24,152},{32,160},{40,168},{48,176},{56,1... | collective-permute-start | bytes 98312 | tf_op jit(solution)/shard_map/ppermute | solution.py:19
  288.4 4.2 collective-permute-start.10
  294.6 3.7 collective-permute-done.11
  298.5 4.2 fusion.16
  302.7 8.6 %fusion.81 = f32[2,64,64,64,1]{3,2,0,1,4:T(8,128)S(1)} fusion(f32[2,64,64,64,1]{3,2,1,0,4:T(8,128)S(1)} %fusion.16, f32[1,2,64,64]{3,2,1,0:T(8,128)S(1)} %get-tuple-element.39, f32[1,2,64,64]{3,2,1,0:T(8,128)S(1)} %get-tuple-element.42), kind=kOutput, calls=%fused_computation.91 | convolution fusion | flops 805322752 | bytes 4259840 | tf_op jit(solution)/shard_map/pqkn,qsnbc->psbck/dot_general | solution.py:47
  311.4 8.9 %fusion.84 = f32[2,64,64,64,1]{3,2,0,1,4:T(8,128)S(1)} fusion(f32[2,64,64,64,1]{3,2,0,1,4:T(8,128)S(1)} %fusion.81, f32[1,2,64,64]{3,2,1,0:T(8,128)S(1)} %get-tuple-element.39, f32[1,2,64,64]{3,2,1,0:T(8,128)S(1)} %get-tuple-element.42), kind=kOutput, calls=%fused_computation.92 | convolution fusion | flops 805322752 | bytes 4259840 | tf_op jit(solution)/shard_map/pqkn,qsnbc->psbck/dot_general | solution.py:47
  320.3 9.1 %fusion.87 = f32[2,1,64,64,64]{4,3,0,2,1:T(8,128)S(1)} fusion(f32[2,64,64,64,1]{3,2,0,1,4:T(8,128)S(1)} %fusion.84, f32[1,2,64,64]{3,2,1,0:T(8,128)S(1)} %get-tuple-element.39, f32[1,2,64,64]{3,2,1,0:T(8,128)S(1)} %get-tuple-element.42), kind=kOutput, calls=%fused_computation.93 | convolution fusion | flops 805322752 | bytes 4259840 | tf_op jit(solution)/shard_map/pqkn,qsnbc->psbck/dot_general | solution.py:47
  331.4 8.7 %fusion.90 = f32[2,64,64,64,1]{3,2,0,1,4:T(8,128)S(1)} fusion(f32[2,64,64,64,1]{3,2,0,1,4:T(8,128)S(1)} %maximum_bitcast_fusion.4, f32[1,2,64,64]{3,2,1,0:T(8,128)S(1)} %get-tuple-element.43, f32[1,2,64,64]{3,2,1,0:T(8,128)S(1)} %get-tuple-element.38), kind=kOutput, calls=%fused_computation.94 | convolution fusion | flops 805322752 | bytes 4259840 | tf_op jit(solution)/shard_map/pqkn,qsnbc->psbck/dot_general | solution.py:47
  340.1 11.7 %fusion.93 = f32[2,64,64,64]{3,2,0,1:T(8,128)} fusion(f32[2,64,64,64,1]{3,2,0,1,4:T(8,128)S(1)} %fusion.90, f32[1,2,64,64]{3,2,1,0:T(8,128)S(1)} %get-tuple-element.43, f32[1,2,64,64]{3,2,1,0:T(8,128)S(1)} %get-tuple-element.38), kind=kOutput, calls=%fused_computation.95 | convolution fusion | flops 805322752 | bytes 4259840 | tf_op jit(solution)/shard_map/pqkn,qsnbc->psbck/dot_general | solution.py:47
  351.8 5.6 %copy.82 = f32[2,64,64,64]{1,3,0,2:T(8,128)} copy(f32[2,64,64,64]{3,2,0,1:T(8,128)} %fusion.93) | data formatting | bytes 4194304 | tf_op jit(solution)/shard_map/reshape.72
  357.4 6.9 %bitcast_subtract_fusion = f32[2,1,64,64,64]{4,3,2,1,0:T(8,128)S(1)} fusion(f32[2,1,64,64,64]{4,3,2,1,0:T(8,128)} %copy-done.4, f32[2,64,64,64]{1,3,0,2:T(8,128)} %copy.82, f32[1,2,64,64]{3,2,1,0:T(8,128)S(1)} %get-tuple-element.43, f32[1,2,64,64]{3,2,1,0:T(8,128)S(1)} %get-tuple-element.38), kind=kOutput, calls=%fused_computation.45 | convolution fusion | flops 805847040 | bytes 6356992 | tf_op jit(solution)/shard_map/pqkn,qsnbc->psbck/dot_general | solution.py:47
  364.4 3.7 fusion.137
  368.1 1.9 maximum_subtract_fusion.3
  370.3 2.3 fusion.102
  372.6 6.3 %fusion.7 = f32[2,1,1,64,64,64]{5,4,3,2,1,0:T(8,128)} fusion(f32[1,1,1,64,64,64]{5,4,3,2,1,0:T(8,128)} %bitcast.385, f32[1,1,1,64,64,64]{5,4,3,2,1,0:T(8,128)S(1)} %bitcast.380, f32[1,1,1,64,64,64]{5,4,3,2,1,0:T(8,128)} %bitcast.392, f32[1,1,1,64,64,64]{5,4,3,2,1,0:T(8,128)} %bitcast.389, f32[1,1,1,64,64,64]{5,4,3,2,1,0:T(8,128)} %get-tuple-element.10, ...), kind=kLoop, calls=%fused_computation.27 | loop fusion | flops 2621440 | bytes 8388608 | tf_op jit(solution)/shard_map/sub | solution.py:144
  378.9 79.9 %reduce-scatter.2.cloned.1.call-done = f32[8,64,64]{2,1,0:T(8,128)} async-done(((f32[64,64,64]{2,1,0:T(8,128)}), f32[8,64,64]{2,1,0:T(8,128)}) %reduce-scatter.2.cloned.1.call-update) | async-done | bytes 131088 | tf_op jit(solution)/shard_map/reduce_scatter | solution.py:147
  (88 shorter events, 31.5 us)
Async XLA Ops:
  7.2 451.6 %reduce-scatter.2.cloned.1.call-start = ((), (), s32[]{:S(2)}) async-start(), calls=%async_computation.1 | async-start | bytes 2359296 | tf_op jit(solution)/shard_map/reduce_scatter | solution.py:147
  143.8 8.6 %copy-start.11 = (f32[1,64,64,64]{3,2,1,0:T(8,128)S(1)}, f32[1,64,64,64]{3,2,1,0:T(8,128)}, u32[]{:S(2)}) copy-start(f32[1,64,64,64]{3,2,1,0:T(8,128)} %param.4) | copy-start | bytes 3145732
  156.0 14.3 %copy-start = (f32[1,64,64,64]{3,2,1,0:T(8,128)}, f32[1,64,64,64]{3,2,1,0:T(8,128)S(1)}, u32[]{:S(2)}) copy-start(f32[1,64,64,64]{3,2,1,0:T(8,128)S(1)} %get-tuple-element.14) | copy-start | bytes 3145732
  156.7 37.5 %collective-permute-start = (f32[2,1,64,64]{3,2,0,1:T(8,128)}, f32[2,1,64,64]{3,2,0,1:T(8,128)}, u32[]{:S(2)}, u32[]{:S(2)}) collective-permute-start(f32[2,1,64,64]{3,2,0,1:T(8,128)} %get-tuple-element.29), channel_id=1, source_target_pairs={{0,128},{8,136},{16,144},{24,152},{32,160},{40,168},{48,176},{56,1... | collective-permute-start | bytes 98312 | tf_op jit(solution)/shard_map/ppermute | solution.py:19
  161.3 35.7 %collective-permute-start.1 = (f32[2,1,64,64]{3,2,0,1:T(8,128)S(1)}, f32[2,1,64,64]{3,2,0,1:T(8,128)}, u32[]{:S(2)}, u32[]{:S(2)}) collective-permute-start(f32[2,1,64,64]{3,2,0,1:T(8,128)S(1)} %get-tuple-element.30), channel_id=1, source_target_pairs={{128,0},{136,8},{144,16},{152,24},{160,32},{168,40},{176,48},{184,... | collective-permute-start | bytes 98312 | tf_op jit(solution)/shard_map/ppermute | solution.py:19
  163.4 34.5 %collective-permute-start.2 = (f32[2,1,64,64]{3,2,0,1:T(8,128)}, f32[2,1,64,64]{3,2,0,1:T(8,128)}, u32[]{:S(2)}, u32[]{:S(2)}) collective-permute-start(f32[2,1,64,64]{3,2,0,1:T(8,128)} %bitcast.59), channel_id=1, source_target_pairs={{0,32},{8,40},{16,48},{24,56},{32,64},{40,72},{48,80},{56,88},{64,... | collective-permute-start | bytes 98312 | tf_op jit(solution)/shard_map/ppermute | solution.py:19
  169.1 29.7 %collective-permute-start.3 = (f32[2,1,64,64]{3,2,0,1:T(8,128)}, f32[2,1,64,64]{3,2,0,1:T(8,128)}, u32[]{:S(2)}, u32[]{:S(2)}) collective-permute-start(f32[2,1,64,64]{3,2,0,1:T(8,128)} %bitcast.61), channel_id=1, source_target_pairs={{32,0},{40,8},{48,16},{56,24},{64,32},{72,40},{80,48},{88,56},{96,... | collective-permute-start | bytes 98312 | tf_op jit(solution)/shard_map/ppermute | solution.py:19
  174.7 24.9 %collective-permute-start.4 = (f32[2,1,64,64]{3,2,0,1:T(8,128)}, f32[2,1,64,64]{3,2,0,1:T(8,128)}, u32[]{:S(2)}, u32[]{:S(2)}) collective-permute-start(f32[2,1,64,64]{3,2,0,1:T(8,128)} %bitcast.207), channel_id=1, source_target_pairs={{0,8},{8,16},{16,24},{24,32},{32,40},{40,48},{48,56},{56,64},{64,7... | collective-permute-start | bytes 98312 | tf_op jit(solution)/shard_map/ppermute | solution.py:19
  190.0 4.2 copy-start.16
  190.0 10.6 %copy-start.1 = (f32[1,64,64,64]{3,2,1,0:T(8,128)S(1)}, f32[1,64,64,64]{3,2,1,0:T(8,128)}, u32[]{:S(2)}) copy-start(f32[1,64,64,64]{3,2,1,0:T(8,128)} %copy-done) | copy-start | bytes 3145732
  190.0 10.6 %copy-start.9 = (f32[2,64,64,64]{3,2,1,0:T(8,128)S(1)}, f32[2,64,64,64]{3,2,1,0:T(8,128)}, u32[]{:S(2)}) copy-start(f32[2,64,64,64]{3,2,1,0:T(8,128)} %constant_dynamic-update-slice_fusion) | copy-start | bytes 6291460
  194.2 6.4 %collective-permute-start.5 = (f32[2,1,64,64]{3,2,0,1:T(8,128)S(1)}, f32[2,1,64,64]{3,2,0,1:T(8,128)S(1)}, u32[]{:S(2)}, u32[]{:S(2)}) collective-permute-start(f32[2,1,64,64]{3,2,0,1:T(8,128)S(1)} %bitcast.396), channel_id=1, source_target_pairs={{8,0},{16,8},{24,16},{32,24},{40,32},{48,40},{56,48},{64,56},{72,6... | collective-permute-start | bytes 98312 | tf_op jit(solution)/shard_map/ppermute | solution.py:19
  261.1 7.1 %copy-start.12 = (f32[1,64,64,64]{3,2,1,0:T(8,128)S(1)}, f32[1,64,64,64]{3,2,1,0:T(8,128)}, u32[]{:S(2)}) copy-start(f32[1,64,64,64]{3,2,1,0:T(8,128)} %param.4) | copy-start | bytes 3145732
  268.2 1.6 copy-start.2
  269.0 29.4 %copy-start.5 = (f32[1,64,64,64]{3,2,1,0:T(8,128)}, f32[1,64,64,64]{3,2,1,0:T(8,128)S(1)}, u32[]{:S(2)}) copy-start(f32[1,64,64,64]{3,2,1,0:T(8,128)S(1)} %get-tuple-element.12) | copy-start | bytes 3145732
  269.0 29.4 %copy-start.7 = (f32[1,64,64,64]{3,2,1,0:T(8,128)}, f32[1,64,64,64]{3,2,1,0:T(8,128)S(1)}, u32[]{:S(2)}) copy-start(f32[1,64,64,64]{3,2,1,0:T(8,128)S(1)} %get-tuple-element.13) | copy-start | bytes 3145732
  271.2 27.2 %copy-start.4 = (f32[2,1,64,64,64]{4,3,2,1,0:T(8,128)}, f32[2,1,64,64,64]{4,3,2,1,0:T(8,128)S(1)}, u32[]{:S(2)}) copy-start(f32[2,1,64,64,64]{4,3,2,1,0:T(8,128)S(1)} %maximum_subtract_fusion.1) | copy-start | bytes 6291460
  274.7 23.8 %copy-start.10 = (f32[2,64,64,64]{3,2,1,0:T(8,128)S(1)}, f32[2,64,64,64]{3,2,1,0:T(8,128)}, u32[]{:S(2)}) copy-start(f32[2,64,64,64]{3,2,1,0:T(8,128)} %constant_dynamic-update-slice_fusion) | copy-start | bytes 6291460
  274.7 23.8 %copy-start.14 = (f32[64,64,64]{2,1,0:T(8,128)S(1)}, f32[64,64,64]{2,1,0:T(8,128)}, u32[]{:S(2)}) copy-start(f32[64,64,64]{2,1,0:T(8,128)} %get-tuple-element.33) | copy-start | bytes 3145732
  275.1 17.5 %collective-permute-start.8 = (f32[2,1,64,64]{3,2,0,1:T(8,128)S(1)}, f32[2,1,64,64]{3,2,0,1:T(8,128)S(1)}, u32[]{:S(2)}, u32[]{:S(2)}) collective-permute-start(f32[2,1,64,64]{3,2,0,1:T(8,128)S(1)} %bitcast.401), channel_id=1, source_target_pairs={{0,32},{8,40},{16,48},{24,56},{32,64},{40,72},{48,80},{56,88},{64,... | collective-permute-start | bytes 98312 | tf_op jit(solution)/shard_map/ppermute | solution.py:19
  280.9 17.5 %collective-permute-start.6 = (f32[2,1,64,64]{3,2,0,1:T(8,128)S(1)}, f32[2,1,64,64]{3,2,0,1:T(8,128)S(1)}, u32[]{:S(2)}, u32[]{:S(2)}) collective-permute-start(f32[2,1,64,64]{3,2,0,1:T(8,128)S(1)} %get-tuple-element.23), channel_id=1, source_target_pairs={{0,128},{8,136},{16,144},{24,152},{32,160},{40,168},{48,176},{56,1... | collective-permute-start | bytes 98312 | tf_op jit(solution)/shard_map/ppermute | solution.py:19
  285.8 12.6 %collective-permute-start.7 = (f32[2,1,64,64]{3,2,0,1:T(8,128)S(1)}, f32[2,1,64,64]{3,2,0,1:T(8,128)S(1)}, u32[]{:S(2)}, u32[]{:S(2)}) collective-permute-start(f32[2,1,64,64]{3,2,0,1:T(8,128)S(1)} %get-tuple-element.24), channel_id=1, source_target_pairs={{128,0},{136,8},{144,16},{152,24},{160,32},{168,40},{176,48},{184,... | collective-permute-start | bytes 98312 | tf_op jit(solution)/shard_map/ppermute | solution.py:19
  287.1 7.5 %collective-permute-start.9 = (f32[2,1,64,64]{3,2,0,1:T(8,128)S(1)}, f32[2,1,64,64]{3,2,0,1:T(8,128)S(1)}, u32[]{:S(2)}, u32[]{:S(2)}) collective-permute-start(f32[2,1,64,64]{3,2,0,1:T(8,128)S(1)} %bitcast.399), channel_id=1, source_target_pairs={{32,0},{40,8},{48,16},{56,24},{64,32},{72,40},{80,48},{88,56},{96,... | collective-permute-start | bytes 98312 | tf_op jit(solution)/shard_map/ppermute | solution.py:19
  288.4 6.2 %collective-permute-start.10 = (f32[2,1,64,64]{3,2,0,1:T(8,128)S(1)}, f32[2,1,64,64]{3,2,0,1:T(8,128)S(1)}, u32[]{:S(2)}, u32[]{:S(2)}) collective-permute-start(f32[2,1,64,64]{3,2,0,1:T(8,128)S(1)} %bitcast.398), channel_id=1, source_target_pairs={{0,8},{8,16},{16,24},{24,32},{32,40},{40,48},{48,56},{56,64},{64,7... | collective-permute-start | bytes 98312 | tf_op jit(solution)/shard_map/ppermute | solution.py:19
  292.6 5.7 %collective-permute-start.11 = (f32[2,1,64,64]{3,2,0,1:T(8,128)S(1)}, f32[2,1,64,64]{3,2,0,1:T(8,128)S(1)}, u32[]{:S(2)}, u32[]{:S(2)}) collective-permute-start(f32[2,1,64,64]{3,2,0,1:T(8,128)S(1)} %bitcast.397), channel_id=1, source_target_pairs={{8,0},{16,8},{24,16},{32,24},{40,32},{48,40},{56,48},{64,56},{72,6... | collective-permute-start | bytes 98312 | tf_op jit(solution)/shard_map/ppermute | solution.py:19
  357.4 6.9 %copy-start.13 = (f32[1,64,64,64]{3,2,1,0:T(8,128)S(1)}, f32[1,64,64,64]{3,2,1,0:T(8,128)}, u32[]{:S(2)}) copy-start(f32[1,64,64,64]{3,2,1,0:T(8,128)} %param.4) | copy-start | bytes 3145732
  364.4 3.7 copy-start.3
  364.4 3.7 copy-start.6
  364.4 3.7 copy-start.8
  368.1 2.2 copy-start.15
Sparse Core Ops, SparseCore 0:
  372.7 86.0 reduce-scatter.1
where the time goes:
time: 471 us; the launch traced here: 466 us
  matrix products  159 us (34%)
  other arithmetic  108 us (23%)
  waiting for transfers between devices  83.7 us (18%)
  local copies, waits for them, and re-layouts  61.7 us (13%)
  starting transfers between devices  38.7 us (8%)
  between operations  14.9 us (3%)
    dot_general x18, matrix products, transform(): jnp.einsum('pqkn,qsnbc->psbck', matrix, values, precision=highest, prefer...  159 us
    reduce_scatter x1, waiting for transfers between devices, local(): lax.psum_scatter(partial_sum, 'src', scatter_dimension=0, tiled=True)  79.9 us
    scatter-add x2, other arithmetic, place(): jax.ops.segment_sum(weights.reshape(-1), segment_ids.reshape(-1), num_seg...  56.4 us
    ppermute x12, starting transfers between devices, shifted_2(): return lax.ppermute(block, axis, route)  38.7 us
    slice x1, local copies, waits for them, and re-layouts, place(): summed.reshape(sources, cube + 1)[:, :cube]  16.3 us
    another operation x7, local copies, waits for them, and re-layouts, local(): source = jnp.stack([place(source_weights[0]), place(source_weights[1])])  15.2 us
    another operation x2, local copies, waits for them, and re-layouts  11.3 us
    reshape x2, local copies, waits for them, and re-layouts, place(): summed.reshape(sources, cube + 1)[:, :cube]  10.6 us
  transfers between devices with their start and end apart: 13, of which 2 were waited for; matrix products, arithmetic and copies ran while one was open for 7% of the time, Pallas kernels for 0%

commit v1 on v0

v1 whole, which is shorter than its diff:
```python
import functools

import jax
import jax.numpy as jnp
import numpy as np
from jax import lax
from jax.experimental import pallas as pl
from jax.experimental.pallas import tpu as pltpu
from jax.sharding import PartitionSpec as P

N = 64
ROWS = N * N
LANES = 2 * N
TERMS = 2
BGX, BGY, BGZ = 2, 4, 4
SRC = 8
SLAB = N // SRC
CH = SLAB * N
DAMP = 0.25
MESH = pl.DeviceIdType.MESH
SLOTS = 256
F32, BF16 = jnp.float32, jnp.bfloat16


def split(values):
    high = values.astype(BF16)
    low = (values - high.astype(F32)).astype(BF16)
    return high, low


def dft_table(sign):
    k = np.arange(N)
    phase = 2.0 * np.pi / N * (k[:, None] * k[None, :] % N)
    c, s = np.cos(phase), sign * np.sin(phase)
    w = np.block([[c, s], [-s, c]]).astype(np.float32)
    high = w.astype(BF16)
    low = (w - high.astype(np.float32)).astype(BF16)
    half = np.concatenate([high, low], axis=1)
    return np.concatenate([half, half], axis=0)


def along_lanes(values, table):
    high, low = split(values)
    out = jnp.dot(jnp.concatenate([high, low], axis=1), table, preferred_element_type=F32)
    return out[:, :LANES] + out[:, LANES:]


def swapped(values):
    lower = lax.broadcasted_iota(jnp.int32, (N, LANES), 1) < N
    blocks = []
    for start in range(0, values.shape[0], LANES):
        turned = values[start : start + LANES].T
        re, im = turned[:N], turned[N:]
        blocks.append(jnp.where(lower, re, pltpu.roll(im, N, 1)))
        blocks.append(jnp.where(lower, pltpu.roll(re, N, 1), im))
    return jnp.concatenate(blocks, axis=0)


def place_kernel(box_ref, cells_ref, wre_ref, wim_ref, out_ref, pos_ref, feat_ref):
    cells = cells_ref[...] - box_ref[0] * (N * N * N)
    inside = (cells >= 0) & (cells < N * N * N)
    mask = jnp.where(inside, 1.0, 0.0).astype(BF16)
    groups = cells.shape[0]
    i0 = lax.broadcasted_iota(jnp.int32, (128, 128), 0)
    i1 = lax.broadcasted_iota(jnp.int32, (128, 128), 1)
    upper = jnp.where(i0 < i1, 1.0, 0.0).astype(BF16)
    within = jnp.dot(mask, upper, preferred_element_type=F32)
    totals = jnp.dot(mask, jnp.ones((128, 128), BF16), preferred_element_type=F32)
    j0 = lax.broadcasted_iota(jnp.int32, (groups, groups), 0)
    j1 = lax.broadcasted_iota(jnp.int32, (groups, groups), 1)
    before = jnp.where(j1 < j0, 1.0, 0.0).astype(BF16)
    offset = jnp.dot(before, totals.astype(BF16), preferred_element_type=F32)
    pos_ref[...] = jnp.where(inside, (within + offset).astype(jnp.int32), -1)
    count = jnp.sum(jnp.where(inside, 1, 0))
    safe = jnp.where(inside, cells, 0)
    rh, rl = split(wre_ref[...])
    ih, il = split(wim_ref[...])
    rows = (
        (safe // ROWS).astype(F32),
        (safe // N % N).astype(F32),
        (safe % N).astype(F32),
        rh.astype(F32),
        rl.astype(F32),
        ih.astype(F32),
        il.astype(F32),
    )
    for n, row in enumerate(rows):
        feat_ref[n] = row

    def chunk(step, carry):
        slot = lax.broadcasted_iota(jnp.int32, (SLOTS, 128), 0) + step * SLOTS
        sub = lax.broadcasted_iota(jnp.int32, (16, 128), 0)
        hots, feats = [], []
        for g in range(groups):
            hots.append(jnp.where(pos_ref[g : g + 1, :] == slot, 1.0, 0.0).astype(BF16))
            f = jnp.zeros((16, 128), F32)
            for n in range(len(rows)):
                f = jnp.where(sub == n, feat_ref[n, g : g + 1, :], f)
            feats.append(f.astype(BF16))
        hot = jnp.concatenate(hots, axis=1)
        feat = jnp.concatenate(feats, axis=1)
        nt = (((1,), (1,)), ((), ()))
        by_lane = lax.dot_general(feat, hot, nt, preferred_element_type=F32)
        by_row = lax.dot_general(hot, feat, nt, preferred_element_type=F32)
        used = lax.broadcasted_iota(jnp.int32, (1, SLOTS), 1) + step * SLOTS < count
        plane = (by_lane[0:1] * N + by_lane[1:2]).astype(jnp.int32)
        plane = jnp.where(used, plane, -1)
        lane = lax.broadcasted_iota(jnp.int32, (SLOTS, LANES), 1)
        hit = lane % N == by_row[:, 2:3].astype(jnp.int32)
        first = lane < N
        high = jnp.where(hit, jnp.where(first, by_row[:, 3:4], by_row[:, 5:6]), 0.0)
        low = jnp.where(hit, jnp.where(first, by_row[:, 4:5], by_row[:, 6:7]), 0.0)
        spread = jnp.concatenate([high, low], axis=1).astype(BF16)

        def rows_of(block, inner):
            start = pl.multiple_of(block * 512, 512)
            at = lax.broadcasted_iota(jnp.int32, (512, SLOTS), 0) + start
            pick = jnp.where(at == plane, 1.0, 0.0).astype(BF16)
            got = jnp.dot(pick, spread, preferred_element_type=F32)
            got = got[:, :LANES] + got[:, LANES:]
            old = out_ref[pl.ds(start, 512), :]
            out_ref[pl.ds(start, 512), :] = jnp.where(step > 0, old, 0.0) + got
            return inner

        return lax.fori_loop(0, ROWS // 512, rows_of, carry)

    lax.fori_loop(0, jnp.maximum(1, (count + SLOTS - 1) // SLOTS), chunk, 0)


def place(box, cells, weights):
    groups = cells.shape[-1] // 128
    return pl.pallas_call(
        place_kernel,
        out_shape=jax.ShapeDtypeStruct((ROWS, LANES), F32),
        in_specs=[pl.BlockSpec(memory_space=pltpu.SMEM)]
        + [pl.BlockSpec(memory_space=pltpu.VMEM)] * 3,
        out_specs=pl.BlockSpec(memory_space=pltpu.VMEM),
        scratch_shapes=[pltpu.VMEM((groups, 128), jnp.int32), pltpu.VMEM((8, groups, 128), F32)],
    )(
        box,
        cells.reshape(groups, 128),
        weights[0].reshape(groups, 128),
        weights[1].reshape(groups, 128),
    )


def series_kernel(
    remote,
    eig_ref, pair_ref, fwd_ref, inv_ref, medium_ref, source_ref, adjoint_ref,
    out_ref, grad_ref,
    field, drive, one, two, kre, kim, faces, zcor, recv, gsend, grecv,
    send_sem, recv_sem, gsend_sem, grecv_sem, out_sem,
):
    if remote:
        space, me = lax.axis_index("space"), lax.axis_index("src")
        bx, by, bz = space // (BGY * BGZ), space // BGZ % BGY, space % BGZ
        below = (
            lax.rem(bx + BGX - 1, BGX) * (BGY * BGZ) + by * BGZ + bz,
            bx * (BGY * BGZ) + lax.rem(by + BGY - 1, BGY) * BGZ + bz,
            bx * (BGY * BGZ) + by * BGZ + lax.rem(bz + BGZ - 1, BGZ),
        )
        above = (
            lax.rem(bx + 1, BGX) * (BGY * BGZ) + by * BGZ + bz,
            bx * (BGY * BGZ) + lax.rem(by + 1, BGY) * BGZ + bz,
            bx * (BGY * BGZ) + by * BGZ + lax.rem(bz + 1, BGZ),
        )
        has_below = [(v > 0).astype(F32) for v in (bx, by, bz)]
        has_above = [(v < e - 1).astype(F32) for v, e in ((bx, BGX), (by, BGY), (bz, BGZ))]
        barrier = pltpu.get_barrier_semaphore()
        for d in range(3):
            for other in (below[d], above[d]):
                pl.semaphore_signal(barrier, 1, device_id={"space": other}, device_id_type=MESH)
        for k in range(1, SRC):
            pl.semaphore_signal(
                barrier, 1, device_id={"src": lax.rem(me + k, SRC)}, device_id_type=MESH
            )
    else:
        me = 0

    wide = lax.broadcasted_iota(jnp.int32, (CH, LANES), 1) < N
    lower = lax.broadcasted_iota(jnp.int32, (N, LANES), 1) < N

    def table(z, carry):
        rows = pl.ds(pl.multiple_of(z * N, N), N)
        shifted = pair_ref[...] + eig_ref[z]
        scale = 1.0 / ((shifted * shifted + DAMP * DAMP) * float(N**3))
        kre[rows, :] = shifted * scale
        kim[rows, :] = jnp.where(lower, -DAMP, DAMP) * scale
        return carry

    lax.fori_loop(0, N, table, 0)
    field[...] = jnp.zeros_like(field)
    zcor[...] = jnp.zeros_like(zcor)

    if remote:
        pl.semaphore_wait(barrier, 6 + SRC - 1)

    def chunk_rows(i):
        return pl.ds(pl.multiple_of(i * CH, CH), CH)

    def forward(origin):
        def z_pass(i, carry):
            rows = chunk_rows(i)
            values = origin[rows, :]
            at = lax.broadcasted_iota(jnp.int32, (LANES, LANES), 0)
            extra = []
            for p in range(SLAB // 2):
                pair = i * (SLAB // 2) + p
                block = jnp.zeros((LANES, LANES), F32)
                for face in range(2):
                    for part in range(2):
                        line = zcor[face, pl.ds(part * (N // 2) + pair, 1), :]
                        block = jnp.where(at == part * N + face * (N - 1), line, block)
                extra.append(block.T)
            values = values + jnp.concatenate(extra, axis=0)
            one[rows, :] = swapped(along_lanes(values, fwd_ref[...]))
            return carry

        lax.fori_loop(0, SRC, z_pass, 0)

    def middle():
        def xy_pass(i, carry):
            rows = chunk_rows(i)
            parts = [one[pl.ds(i * SLAB + z, N, stride=N), :] for z in range(SLAB)]
            values = along_lanes(jnp.concatenate(parts, axis=0), fwd_ref[...])
            values = along_lanes(swapped(values), fwd_ref[...])
            values = kre[rows, :] * values + kim[rows, :] * pltpu.roll(values, N, 1)
            values = swapped(along_lanes(values, inv_ref[...]))
            values = along_lanes(values, inv_ref[...])
            for z in range(SLAB):
                two[pl.ds(i * SLAB + z, N, stride=N), :] = values[z * N : (z + 1) * N]
            return carry

        lax.fori_loop(0, SRC, xy_pass, 0)

    def updated(rows):
        green = along_lanes(swapped(two[rows, :]), inv_ref[...])
        plain = medium_ref[rows, :] - 1.0
        potential = jnp.concatenate([plain, plain], axis=1)
        ratio = jnp.where(wide, -1.0 / DAMP, 1.0 / DAMP) * potential
        new = green - ratio * pltpu.roll(field[rows, :] - green, N, 1)
        return new, potential

    def term(step, carry):
        forward(drive)
        middle()

        def z_pass(i, inner):
            rows = chunk_rows(i)
            new, potential = updated(rows)
            field[rows, :] = new
            turn = jnp.where(wide, DAMP, -DAMP) * pltpu.roll(new, N, 1)
            drive[rows, :] = potential * new + turn + source_ref[rows, :]
            for p in range(SLAB // 2):
                pair = i * (SLAB // 2) + p
                block = new[p * LANES : (p + 1) * LANES].T
                for face in range(2):
                    for part in range(2):
                        line = part * N + face * (N - 1)
                        faces[2 + face, pl.ds(part * (N // 2) + pair, 1), :] = block[line : line + 1]
            return inner

        lax.fori_loop(0, SRC, z_pass, 0)
        first, last = pl.ds(0, N), pl.ds(ROWS - N, N)
        y_first, y_last = pl.ds(0, N, stride=N), pl.ds(N - 1, N, stride=N)
        faces[0] = field[y_first, :]
        faces[1] = field[y_last, :]
        if remote:
            sends = (
                (field.at[first], field.at[last]),
                (faces.at[0], faces.at[1]),
                (faces.at[2], faces.at[3]),
            )
            copies = []
            for d in range(3):
                for side, other in ((1, above[d]), (0, below[d])):
                    slot = 2 * d + 1 - side
                    copies.append(
                        pltpu.make_async_remote_copy(
                            src_ref=sends[d][side],
                            dst_ref=recv.at[step, slot],
                            send_sem=send_sem.at[step, slot],
                            recv_sem=recv_sem.at[step, slot],
                            device_id={"space": other},
                            device_id_type=MESH,
                        )
                    )
            for copy in copies:
                copy.start()
            for copy in copies:
                copy.wait()
            got = [[m * recv[step, 2 * d + s] for s, m in ((0, has_below[d]), (1, has_above[d]))] for d in range(3)]
        else:
            got = [[0.0, 0.0]] * 3
        drive[first, :] = drive[first, :] + (got[0][0] - field[last, :])
        drive[last, :] = drive[last, :] + (got[0][1] - field[first, :])
        drive[y_first, :] = drive[y_first, :] + (got[1][0] - faces[1])
        drive[y_last, :] = drive[y_last, :] + (got[1][1] - faces[0])
        zcor[0] = got[2][0] - faces[3]
        zcor[1] = got[2][1] - faces[2]
        return carry

    drive[...] = source_ref[...]
    lax.fori_loop(0, TERMS, term, 0)

    forward(drive)
    middle()

    def grad_copy(owner, slot):
        return pltpu.make_async_remote_copy(
            src_ref=gsend.at[owner],
            dst_ref=grecv.at[slot],
            send_sem=gsend_sem.at[owner],
            recv_sem=grecv_sem.at[slot],
            device_id={"src": owner},
            device_id_type=MESH,
        )

    def out_copy(i):
        rows = chunk_rows(i)
        return pltpu.make_async_copy(field.at[rows], out_ref.at[rows], out_sem.at[i])

    def last_pass(k, carry):
        i = lax.rem(me + 1 + k, SRC)
        rows = chunk_rows(i)
        new, _ = updated(rows)
        field[rows, :] = new
        out_copy(i).start()
        both = jnp.concatenate([adjoint_ref[0, rows, :], adjoint_ref[1, rows, :]], axis=1)
        terms = both.astype(F32) * new
        terms = terms - pltpu.roll(terms, N, 1)
        half = CH // 2
        gsend[i] = jnp.where(wide[:half], terms[:half], -terms[half:])
        if remote:

            @pl.when(k < SRC - 1)
            def _():
                grad_copy(i, me).start()

        return carry

    lax.fori_loop(0, SRC, last_pass, 0)
    total = gsend[me]
    if remote:
        for k in range(1, SRC):
            other = lax.rem(me + k, SRC)
            grad_copy(other, other).wait_recv()
            total = total + grecv[other]
    grad_ref[0 : CH // 2, :] = total[:, :N]
    grad_ref[CH // 2 :, :] = pltpu.roll(total, N, 1)[:, :N]
    if remote:
        for k in range(1, SRC):
            grad_copy(lax.rem(me + k, SRC), me).wait_send()
    for i in range(SRC):
        out_copy(i).wait()


def series(medium, source, adjoint, remote=True):
    eig = 2.0 - 2.0 * np.cos(2.0 * np.pi / N * np.arange(N))
    both = np.concatenate([eig, eig])
    pair = (eig[:, None] + both[None, :] - 1.0).astype(np.float32)
    big = lambda: pltpu.VMEM((ROWS, LANES), F32)
    face = (N, LANES)
    vmem = pl.BlockSpec(memory_space=pltpu.VMEM)
    return pl.pallas_call(
        functools.partial(series_kernel, remote),
        out_shape=(
            jax.ShapeDtypeStruct((ROWS, LANES), F32),
            jax.ShapeDtypeStruct((CH, N), F32),
        ),
        in_specs=[pl.BlockSpec(memory_space=pltpu.SMEM)] + [vmem] * 6,
        out_specs=(pl.BlockSpec(memory_space=pl.ANY), vmem),
        scratch_shapes=[
            big(), big(), big(), big(), big(), big(),
            pltpu.VMEM((4,) + face, F32),
            pltpu.VMEM((2,) + face, F32),
            pltpu.VMEM((TERMS, 6) + face, F32),
            pltpu.VMEM((SRC, CH // 2, LANES), F32),
            pltpu.VMEM((SRC, CH // 2, LANES), F32),
            pltpu.SemaphoreType.DMA((TERMS, 6)),
            pltpu.SemaphoreType.DMA((TERMS, 6)),
            pltpu.SemaphoreType.DMA((SRC,)),
            pltpu.SemaphoreType.DMA((SRC,)),
            pltpu.SemaphoreType.DMA((SRC,)),
        ],
        compiler_params=pltpu.CompilerParams(
            collective_id=0 if remote else None,
            has_side_effects=remote,
            vmem_limit_bytes=60 * 1024 * 1024,
        ),
    )(
        jnp.asarray(eig.astype(np.float32)),
        jnp.asarray(pair),
        jnp.asarray(dft_table(-1.0)),
        jnp.asarray(dft_table(1.0)),
        medium.reshape(ROWS, N),
        source,
        adjoint.reshape(2, ROWS, N),
    )


def local(medium, source_cells, source_weights, adjoint):
    box = lax.axis_index("space").astype(jnp.int32).reshape(1)
    source = place(box, source_cells, source_weights)
    packed, owned = series(medium, source, adjoint)
    field = packed.reshape(N, N, 2, N).transpose(2, 0, 1, 3)
    return field[:, None, None], owned.reshape(1, SLAB, N, N)


def solution(mesh):
    placed = (
        P("space", None, None, None),
        P("src", None),
        P(None, "src", None),
        P(None, "src", "space", None, None, None),
    )
    return jax.shard_map(
        local,
        mesh=mesh,
        in_specs=placed,
        out_specs=(P(None, "src", "space", None, None, None), P("space", "src", None, None)),
        check_vma=False,
    )
```

time: 471 us -> 113 us (0.24); the launches traced: 466 us -> 113 us
  matrix products: 159 us -> 0 us
  other arithmetic: 108 us -> 0 us
  Pallas kernels: 0 us -> 99.6 us
  waiting for transfers between devices: 83.7 us -> 0 us
  local copies, waits for them, and re-layouts: 61.7 us -> 12.5 us
  starting transfers between devices: 38.7 us -> 0 us
  between operations: 14.9 us -> 0.64 us
    dot_general x18 -> x0, matrix products: 159 us -> none  [transform(): jnp.einsum('pqkn,qsnbc->psbck', matrix, values, precision=highest, prefer...]
    pallas_call x0 -> x2, Pallas kernels: none -> 99.6 us  [the longest x1 94 us: series(): pl.pallas_call(functools.partial(series_kernel, remote), out_shape=(jax.S...]
    reduce_scatter x1 -> x0, waiting for transfers between devices: 79.9 us -> none  [local(): lax.psum_scatter(partial_sum, 'src', scatter_dimension=0, tiled=True)]
    scatter-add x2 -> x0, other arithmetic: 56.4 us -> none  [place(): jax.ops.segment_sum(weights.reshape(-1), segment_ids.reshape(-1), num_seg...]
    ppermute x12 -> x0, starting transfers between devices: 38.7 us -> none  [shifted_2(): return lax.ppermute(block, axis, route)]
    another operation x9 -> x0, local copies, waits for them, and re-layouts: 26.4 us -> none  [the longest x7 15.2 us: local(): source = jnp.stack([place(source_weights[0]), place(source_weights[1])])]
    slice x4 -> x1, local copies, waits for them, and re-layouts: 20.5 us -> 1.35 us  [place(): weights[1].reshape(groups, 128)]
    sub x9 -> x0, other arithmetic: 16.4 us -> none  [the longest x3 9.64 us: local(): field = field - times_gamma(update, ratio)]
  transfers between devices with their start and end apart: 13 -> 0, of which waited for: 2 -> 0; matrix products, arithmetic and copies ran while one was open for 7% -> 0% of each run, Pallas kernels for 0% -> 0%
where the time goes in v1:
time: 113 us
  Pallas kernels  99.6 us (88%)
  local copies, waits for them, and re-layouts  12.5 us (11%)
    pallas_call x1, Pallas kernels, series(): pl.pallas_call(functools.partial(series_kernel, remote), out_shape=(jax.S...  94 us
    reshape x2, local copies, waits for them, and re-layouts, local(): field = packed.reshape(N, N, 2, N).transpose(2, 0, 1, 3)  10.5 us
    pallas_call x1, Pallas kernels, place(): pl.pallas_call(place_kernel, out_shape=jax.ShapeDtypeStruct((ROWS, LANES)...  5.61 us

profile of v1, /device:TPU:1, one launch (start us, length us, event | category | flops | bytes accessed | tf_op | source)
XLA Modules:
  0.0 112.8 jit_solution(11071368201290288763)
XLA Ops:
  0.6 1.3 %fusion = (f32[1,1,4096]{2,1,0:T(1,128)}, f32[1,1,4096]{2,1,0:T(1,128)}) fusion(f32[2,1,4096]{2,1,0:T(1,128)} %param.10), kind=kLoop, calls=%fused_computation.1 | loop fusion | bytes 65536 | tf_op jit(solution)/shard_map/slice | solution.py:143
  2.0 5.6 %shard_map.95.source_ref = f32[4096,128]{1,0:T(8,128)} custom-call(s32[1]{0:T(128)} %bitcast.1.box_ref, s32[32,128]{1,0:T(8,128)} %bitcast.18, f32[32,128]{1,0:T(8,128)} %bitcast.17, f32[32,128]{1,0:T(8,128)} %bitcast.16), custom_call_target="tpu_custom_call" | custom-call | tf_op jit(solution)/shard_map/pallas_call | solution.py:132
  7.6 94.0 %shard_map.96 = (f32[4096,128]{1,0:T(8,128)}, f32[512,64]{1,0:T(8,128)}) custom-call(f32[64]{0:T(128)} %constant.14.clone.eig_ref, f32[64,128]{1,0:T(8,128)} %constant.15.clone.pair_ref, bf16[256,256]{1,0:T(8,128)(2,1)} %constant.16.clone.fwd_ref, bf16[256,256]{1,0:T(8,128)(2,1)} %constant.17.clone.inv_ref, f32[4096,64]{1,0:T(8,128)} %bitcast.13, ...), custom_call_target="tpu_custom_call" | custom-call | tf_op jit(solution)/shard_map/pallas_call | solution.py:365
  101.6 5.6 %reshape.26 = f32[64,64,2,64]{3,2,1,0:T(2,128)} reshape(f32[4096,128]{1,0:T(8,128)} %get-tuple-element.4) | data formatting | bytes 4194304 | tf_op jit(solution)/shard_map/reshape | solution.py:406
  107.2 0.0 copy-start
  107.2 4.8 %copy.12 = f32[64,64,2,64]{3,1,0,2:T(8,128)} copy(f32[64,64,2,64]{3,2,1,0:T(2,128)} %reshape.26) | data formatting | bytes 4194304 | tf_op jit(solution)/shard_map/reshape | solution.py:406
  112.1 0.0 copy-done
  112.1 0.7 copy.14
Async XLA Ops:
  107.2 4.8 %copy-start = (f32[512,64]{1,0:T(8,128)S(1)}, f32[512,64]{1,0:T(8,128)}, u32[]{:S(2)}) copy-start(f32[512,64]{1,0:T(8,128)} %get-tuple-element.5) | copy-start | bytes 393220
